TPU v7x, 32 devices: a whole 2x2x4 slice. The times are simulated.
32 devices in a mesh: win: 4 (over z), sec: 8 (over y, x, core).
Axes of the slice: x: 2, y: 2, z: 4, core: 2. Of those that a mesh axis runs over, the one named last changes fastest.
Arguments:
- initial: bfloat16 [5, 8, 24, 512], P(None, 'win'), may hold values from -6 to 6
- props: bfloat16 [8, 8, 2, 256, 256], P('sec'), may hold values from -0.25 to 0.25
- screen: float32 [8, 8, 256], P('sec', 'win'), may hold values from -3.140625 to 3.140625
- links: int32 [8, 8, 6], P('sec', 'win'), may hold values from 0 to 7, as said below
- kinds: int32 [8, 8, 6], P('sec', 'win'), may hold values from 0 to 7
- counts: int32 [8, 8], P('sec', 'win'), may hold values from 1 to 6
Outputs:
- fields: bfloat16 [8, 5, 8, 24, 512], P('sec', None, 'win')
Inputs may be any that keep to these rules, and one draw needn't show every extreme that they name: links[s, w, l] lies within w - 1 to w + 1.
All inputs are finite; a program needn't handle non-finite values.
Results may differ from a plain program's by a relative error of at most 0.033.
Values may be sent and summed in bfloat16 or wider, within the bound.
A program may use at most 64 MiB of HBM per device.

v0:
```python
import functools

import jax
import jax.numpy as jnp
from jax import lax
from jax.experimental import pallas as pl
from jax.experimental.pallas import tpu as pltpu
from jax.sharding import PartitionSpec as P

MESH = pl.DeviceIdType.MESH


def kernel(
    wins, secs, links, kinds, counts, screen, initial, props, out,
    inbox, table, mixed, coef, turn, table_sem, seed_sem, send_sem, recv_sem,
):
    z = lax.axis_index("win")
    s = lax.axis_index("sec")
    fronts, local, sources, width = initial.shape
    coeffs = width // 2
    entries = props.shape[0]
    length = links.shape[2]
    has_low = z > 0
    has_high = z < wins - 1
    first = s == 0
    sends = s < secs - 1

    loads = [
        pltpu.make_async_copy(props.at[:, part], table.at[part], table_sem.at[part])
        for part in (0, 1)
    ]
    for load in loads:
        load.start()

    barrier = pltpu.get_barrier_semaphore()

    def greet(win, sec):
        pl.semaphore_signal(barrier, inc=1, device_id=(win, sec), device_id_type=MESH)

    @pl.when(s > 0)
    def _():
        greet(z, s - 1)

    @pl.when(has_low)
    def _():
        greet(z - 1, jnp.maximum(s - 1, 0))

    @pl.when(has_high)
    def _():
        greet(z + 1, jnp.maximum(s - 1, 0))

    sides = has_low.astype(jnp.int32) + has_high.astype(jnp.int32)
    expected = jnp.where(sends, 1 + sides, 0) + jnp.where(first, sides, 0)

    @pl.when(expected > 0)
    def _():
        pl.semaphore_wait(barrier, expected)

    def remote(source, target, send, receive, win, sec):
        return pltpu.make_async_remote_copy(
            src_ref=source, dst_ref=target, send_sem=send, recv_sem=receive,
            device_id=(win, sec), device_id_type=MESH,
        )

    def seed_own(f):
        return pltpu.make_async_copy(
            initial.at[f], inbox.at[f, pl.ds(1, local)], recv_sem.at[f, 0]
        )

    def seed_low(f):
        return remote(
            initial.at[f, 0], inbox.at[f, local + 1], seed_sem.at[f, 0], recv_sem.at[f, 2], z - 1, s
        )

    def seed_high(f):
        return remote(
            initial.at[f, local - 1], inbox.at[f, 0], seed_sem.at[f, 1], recv_sem.at[f, 1], z + 1, s
        )

    @pl.when(first & has_low)
    def _():
        for f in range(fronts):
            seed_low(f).start()

    @pl.when(first & has_high)
    def _():
        for f in range(fronts):
            seed_high(f).start()

    @pl.when(first)
    def _():
        for f in range(fronts):
            seed_own(f).start()

    @pl.when(jnp.logical_not(has_low))
    def _():
        inbox[:, 0] = jnp.zeros((fronts, sources, width), jnp.bfloat16)

    @pl.when(jnp.logical_not(has_high))
    def _():
        inbox[:, local + 1] = jnp.zeros((fronts, sources, width), jnp.bfloat16)

    for w in range(local):
        live = counts[0, w]
        codes = []
        for l in range(length):
            offset = links[0, w, l] - (z * local + w - 1)
            codes.append(jnp.where(l < live, kinds[0, w, l] * 3 + offset, -1))
        for code in range(entries * 3):
            hits = sum((c == code).astype(jnp.int32) for c in codes)
            coef[w, code] = hits.astype(jnp.float32)
        scale = lax.rsqrt(jnp.full((1, coeffs), live, jnp.int32).astype(jnp.float32))
        phase = screen[0, pl.ds(w, 1), :]
        turn[w, 0] = jnp.broadcast_to(jnp.cos(phase) * scale, turn.shape[2:])
        turn[w, 1] = jnp.broadcast_to(jnp.sin(phase) * scale, turn.shape[2:])

    for load in loads:
        load.wait()

    def send_own(f):
        return remote(
            out.at[0, f], inbox.at[f, pl.ds(1, local)], send_sem.at[f, 0], recv_sem.at[f, 0], z, s + 1
        )

    def send_low(f):
        return remote(
            out.at[0, f, 0], inbox.at[f, local + 1], send_sem.at[f, 1], recv_sem.at[f, 2], z - 1, s + 1
        )

    def send_high(f):
        return remote(
            out.at[0, f, local - 1], inbox.at[f, 0], send_sem.at[f, 2], recv_sem.at[f, 1], z + 1, s + 1
        )

    def arrived(ref, sem):
        pltpu.make_async_copy(ref, ref, sem).wait()

    depth = entries * coeffs

    def step(f, carry):
        arrived(inbox.at[f, pl.ds(1, local)], recv_sem.at[f, 0])

        @pl.when(has_low)
        def _():
            arrived(inbox.at[f, 0], recv_sem.at[f, 1])

        @pl.when(has_high)
        def _():
            arrived(inbox.at[f, local + 1], recv_sem.at[f, 2])

        held = [inbox[f, j].astype(jnp.float32) for j in range(local + 2)]
        for entry in range(entries):
            stack = []
            for w in range(local):
                total = coef[w, entry * 3] * held[w]
                for d in (1, 2):
                    total = total + coef[w, entry * 3 + d] * held[w + d]
                a, b = total[:, :coeffs], total[:, coeffs:]
                stack += [a, b]
            left = entry * coeffs
            mixed[:, left : left + coeffs] = jnp.concatenate(stack, 0).astype(jnp.bfloat16)
        lhs = mixed[...]
        by_real, by_imag = (
            jnp.dot(lhs, table[part].reshape(depth, coeffs), preferred_element_type=jnp.float32)
            for part in (0, 1)
        )
        for w in range(local):
            top = 2 * w * sources
            mid, low = top + sources, top + 2 * sources
            a = by_real[top:mid] - by_imag[mid:low]
            b = by_real[mid:low] + by_imag[top:mid]
            c = turn[w, 0, :1]
            d = turn[w, 1, :1]
            out[0, f, w, :, :coeffs] = (a * c - b * d).astype(jnp.bfloat16)
            out[0, f, w, :, coeffs:] = (a * d + b * c).astype(jnp.bfloat16)

        @pl.when(f >= 2)
        def _():
            @pl.when(sends & has_low)
            def _():
                send_low(f - 2).wait_send()

            @pl.when(sends & has_high)
            def _():
                send_high(f - 2).wait_send()

            @pl.when(sends)
            def _():
                send_own(f - 2).wait_send()

        @pl.when(sends & has_low)
        def _():
            send_low(f).start()

        @pl.when(sends & has_high)
        def _():
            send_high(f).start()

        @pl.when(sends)
        def _():
            send_own(f).start()

        return carry

    lax.fori_loop(0, fronts, step, 0)

    @pl.when(first & has_low)
    def _():
        for f in range(fronts):
            seed_low(f).wait_send()

    @pl.when(first & has_high)
    def _():
        for f in range(fronts):
            seed_high(f).wait_send()

    @pl.when(sends & has_low)
    def _():
        for f in range(max(fronts - 2, 0), fronts):
            send_low(f).wait_send()

    @pl.when(sends & has_high)
    def _():
        for f in range(max(fronts - 2, 0), fronts):
            send_high(f).wait_send()

    @pl.when(sends)
    def _():
        for f in range(max(fronts - 2, 0), fronts):
            send_own(f).wait_send()


def solution(mesh):
    wins, secs = mesh.shape["win"], mesh.shape["sec"]

    def run(initial, props, screen, links, kinds, counts):
        fronts, local, sources, width = initial.shape
        coeffs = width // 2
        entries = props.shape[1]
        smem = pl.BlockSpec(memory_space=pltpu.SMEM)
        vmem = pl.BlockSpec(memory_space=pltpu.VMEM)
        whole = pl.BlockSpec(memory_space=pl.ANY)
        return pl.pallas_call(
            functools.partial(kernel, wins, secs),
            out_shape=pltpu.VMEM((1, fronts, local, sources, width), jnp.bfloat16),
            in_specs=[smem, smem, smem, vmem, whole, whole],
            out_specs=vmem,
            scratch_shapes=[
                pltpu.VMEM((fronts, local + 2, sources, width), jnp.bfloat16),
                pltpu.VMEM((2, entries, coeffs, coeffs), jnp.bfloat16),
                pltpu.VMEM((2 * local * sources, entries * coeffs), jnp.bfloat16),
                pltpu.SMEM((local, 3 * entries), jnp.float32),
                pltpu.VMEM((local, 2, 8, coeffs), jnp.float32),
                pltpu.SemaphoreType.DMA((2,)),
                pltpu.SemaphoreType.DMA((fronts, 2)),
                pltpu.SemaphoreType.DMA((fronts, 3)),
                pltpu.SemaphoreType.DMA((fronts, 3)),
            ],
            compiler_params=pltpu.CompilerParams(collective_id=0, has_side_effects=True),
            name="beamlets",
        )(links, kinds, counts, screen, initial, props[0])

    placed = (
        P(None, "win", None, None),
        P("sec", None, None, None, None),
        P("sec", "win", None),
        P("sec", "win", None),
        P("sec", "win", None),
        P("sec", "win"),
    )
    return jax.shard_map(
        run,
        mesh=mesh,
        in_specs=placed,
        out_specs=P("sec", None, "win", None, None),
        check_vma=False,
    )
```

profile of v0, /device:TPU:7, one launch (start us, length us, event | category | flops | bytes accessed | tf_op | source)
XLA Modules:
  0.0 36.3 jit_solution(8587860152720736565)
XLA Ops:
  0.0 35.6 %beamlets.1 = bf16[1,5,2,24,512]{4,3,2,1,0:T(8,128)(2,1)S(1)} custom-call(s32[1,2,6]{2,1,0:T(2,128)} %links.1, s32[1,2,6]{2,1,0:T(2,128)} %kinds.1, s32[1,2]{1,0:T(1,128)} %counts.1, f32[1,2,256]{2,1,0:T(2,128)} %screen.1, bf16[5,2,24,512]{3,2,1,0:T(8,128)(2,1)} %initial.1, bf16[8,2,256,256]{3,2,1,0:T(8,128)(2,1)} %bitcast.1), custom_call_target="tpu_custom_call" | custom-call | tf_op jit(solution)/shard_map/beamlets/pallas_call | solution.py:243
  35.6 0.7 %copy.8 = bf16[1,5,2,24,512]{4,3,2,1,0:T(8,128)(2,1)} copy(bf16[1,5,2,24,512]{4,3,2,1,0:T(8,128)(2,1)S(1)} %beamlets.1) | data formatting | bytes 491520
where the time goes:
time: 36.5 us; the launch traced here: 36.3 us
  Pallas kernels  35.6 us (98%)
  local copies, waits for them, and re-layouts  0.7 us (2%)
    pallas_call x1, Pallas kernels, run(): pl.pallas_call(functools.partial(kernel, wins, secs), out_shape=pltpu.VME...  35.6 us

commit v1 on v0

v1 whole, which is shorter than its diff:
```python
import functools

import jax
import jax.numpy as jnp
from jax import lax
from jax.experimental import pallas as pl
from jax.experimental.pallas import tpu as pltpu
from jax.sharding import PartitionSpec as P

MESH = pl.DeviceIdType.MESH
REACH = 2


def kernel(
    wins, secs, group, links, kinds, counts, screen, initial, props, out,
    inbox, stage, table, mixed, meta, table_sem, seed_sem, meta_sem, send_sem, recv_sem,
):
    z = lax.axis_index("win")
    s = lax.axis_index("sec")
    fronts, local, sources, width = initial.shape
    coeffs = width // 2
    entries = props.shape[0]
    length = links.shape[2]
    pieces = sources // group
    wide = local + 2
    even = lax.rem(s, 2) == 0
    odd = jnp.logical_not(even)
    has_low = z > 0
    has_high = z < wins - 1
    first = s == 0
    sends = s < secs - 1
    sides = has_low.astype(jnp.int32) + has_high.astype(jnp.int32)

    loads = [
        pltpu.make_async_copy(props.at[:, part], table.at[part], table_sem.at[part])
        for part in (0, 1)
    ]
    for load in loads:
        load.start()

    barrier = pltpu.get_barrier_semaphore()

    def greet(win, sec):
        pl.semaphore_signal(barrier, inc=1, device_id=(win, sec), device_id_type=MESH)

    def remote(source, target, send, receive, win, sec):
        return pltpu.make_async_remote_copy(
            src_ref=source, dst_ref=target, send_sem=send, recv_sem=receive,
            device_id=(win, sec), device_id_type=MESH,
        )

    def arrived(ref, sem):
        pltpu.make_async_copy(ref, ref, sem).wait()

    @pl.when(even & has_low)
    def _():
        greet(z - 1, s)

    @pl.when(even & has_high)
    def _():
        greet(z + 1, s)

    @pl.when(s > 0)
    def _():
        greet(z, s - 1)

    @pl.when(even & (s > 0) & has_low)
    def _():
        greet(z - 1, s - 1)

    @pl.when(even & (s > 0) & has_high)
    def _():
        greet(z + 1, s - 1)

    def rows_of(g):
        return pl.ds(pl.multiple_of(g * group, group), group)

    @pl.when(first)
    def _():
        for f in range(fronts):
            for g in range(pieces):
                rows = pl.ds(g * group, group)
                pltpu.make_async_copy(
                    initial.at[f, :, rows], inbox.at[f, REACH : REACH + local, rows],
                    recv_sem.at[f * pieces + g],
                ).start()

    @pl.when(even & jnp.logical_not(has_low))
    def _():
        inbox[:, :REACH] = jnp.zeros((fronts, REACH, sources, width), jnp.bfloat16)
        meta[0] = jnp.zeros(meta.shape[1:], jnp.float32)

    @pl.when(even & jnp.logical_not(has_high))
    def _():
        inbox[:, REACH + local :] = jnp.zeros((fronts, REACH, sources, width), jnp.bfloat16)
        meta[local + 1] = jnp.zeros(meta.shape[1:], jnp.float32)

    expected = jnp.where(
        even, sides + sends.astype(jnp.int32), jnp.where(sends, 1 + sides, 0)
    )

    @pl.when(expected > 0)
    def _():
        pl.semaphore_wait(barrier, expected)

    low_seed = (slice(0, REACH), slice(REACH + local, 2 * REACH + local))
    high_seed = (slice(local - REACH, local), slice(0, REACH))

    def seed(f, g, low):
        mine, theirs = low_seed if low else high_seed
        rows = pl.ds(g * group, group)
        return remote(
            initial.at[f, mine, rows], inbox.at[f, theirs, rows], seed_sem,
            recv_sem.at[f * pieces + g], z - 1 if low else z + 1, s,
        )

    @pl.when(first & has_low)
    def _():
        for f in range(fronts):
            for g in range(pieces):
                seed(f, g, True).start()

    @pl.when(first & has_high)
    def _():
        for f in range(fronts):
            for g in range(pieces):
                seed(f, g, False).start()

    codes_at = lax.broadcasted_iota(jnp.int32, (3 * entries, coeffs), 0)
    for w in range(local):
        live = counts[0, w]
        hits = jnp.zeros((3 * entries, coeffs), jnp.float32)
        for l in range(length):
            offset = links[0, w, l] - (z * local + w - 1)
            code = jnp.where(l < live, kinds[0, w, l] * 3 + offset, -1)
            hits = hits + (codes_at == code).astype(jnp.float32)
        meta[w + 1, : 3 * entries] = hits
        scale = lax.rsqrt(jnp.full((1, coeffs), live, jnp.int32).astype(jnp.float32))
        phase = screen[0, pl.ds(w, 1), :]
        meta[w + 1, pl.ds(3 * entries, 1)] = jnp.cos(phase) * scale
        meta[w + 1, pl.ds(3 * entries + 1, 1)] = jnp.sin(phase) * scale

    meta_low = remote(meta.at[1], meta.at[local + 1], meta_sem.at[0], meta_sem.at[1], z - 1, s)
    meta_high = remote(meta.at[local], meta.at[0], meta_sem.at[0], meta_sem.at[1], z + 1, s)

    @pl.when(even & has_low)
    def _():
        meta_low.start()

    @pl.when(even & has_high)
    def _():
        meta_high.start()

    def by_sides(wait):
        for count in (0, 1, 2):
            @pl.when(sides == count)
            def _():
                wait(count)

    def wait_meta(at):
        def wait(count):
            if count:
                arrived(meta.at[:count], meta_sem.at[at])
        return wait

    @pl.when(even)
    def _():
        by_sides(wait_meta(1))

    for load in loads:
        load.wait()

    depth = entries * coeffs

    def section(f, rows, windows, slot):
        held = [inbox[f, j, rows, :].astype(jnp.float32) for j in range(windows + 2)]
        tall = 2 * windows * group
        for entry in range(entries):
            stack = []
            for w in range(windows):
                parts = []
                for half in (0, 1):
                    at = slice(half * coeffs, (half + 1) * coeffs)
                    total = None
                    for d in range(3):
                        term = meta[slot + w, pl.ds(3 * entry + d, 1), :] * held[w + d][:, at]
                        total = term if total is None else total + term
                    parts.append(total)
                stack += parts
            left = entry * coeffs
            mixed[:tall, left : left + coeffs] = jnp.concatenate(stack, 0).astype(jnp.bfloat16)
        lhs = mixed[:tall]
        by_real, by_imag = (
            jnp.dot(lhs, table[part].reshape(depth, coeffs), preferred_element_type=jnp.float32)
            for part in (0, 1)
        )
        results = []
        for w in range(windows):
            top = 2 * w * group
            mid, low = top + group, top + 2 * group
            a = by_real[top:mid] - by_imag[mid:low]
            b = by_real[mid:low] + by_imag[top:mid]
            c = meta[slot + w, pl.ds(3 * entries, 1), :]
            d = meta[slot + w, pl.ds(3 * entries + 1, 1), :]
            results.append(((a * c - b * d).astype(jnp.bfloat16), (a * d + b * c).astype(jnp.bfloat16)))
        return results

    def even_step(u, carry):
        f = u // pieces
        rows = rows_of(u % pieces)

        def wait(count):
            arrived(inbox.at[f, : local + REACH * count, rows], recv_sem.at[u])

        by_sides(wait)
        for w, (a, b) in enumerate(section(f, rows, wide, 0)):
            stage[f, w, rows, :coeffs] = a
            stage[f, w, rows, coeffs:] = b
            if 0 < w <= local:
                out[0, f, w - 1, rows, :coeffs] = a
                out[0, f, w - 1, rows, coeffs:] = b

        @pl.when(sends)
        def _():
            remote(
                stage.at[f, :, rows], inbox.at[f, :wide, rows], send_sem, recv_sem.at[u], z, s + 1
            ).start()

        return carry

    def odd_step(u, carry):
        f = u // pieces
        rows = rows_of(u % pieces)
        arrived(inbox.at[f, :wide, rows], recv_sem.at[u])
        for w, (a, b) in enumerate(section(f, rows, local, 1)):
            out[0, f, w, rows, :coeffs] = a
            out[0, f, w, rows, coeffs:] = b

        def send(mine, theirs, win):
            remote(
                out.at[0, f, mine, rows], inbox.at[f, theirs, rows], send_sem, recv_sem.at[u], win, s + 1
            ).start()

        @pl.when(sends & has_low)
        def _():
            send(*low_seed, z - 1)

        @pl.when(sends & has_high)
        def _():
            send(*high_seed, z + 1)

        @pl.when(sends)
        def _():
            send(slice(0, local), slice(REACH, REACH + local), z)

        return carry

    units = fronts * pieces

    @pl.when(even)
    def _():
        lax.fori_loop(0, units, even_step, 0)

        @pl.when(sends)
        def _():
            arrived(stage, send_sem)

        by_sides(wait_meta(0))

    @pl.when(odd)
    def _():
        lax.fori_loop(0, units, odd_step, 0)

        def wait(count):
            arrived(inbox.at[:, : local + REACH * count], send_sem)

        @pl.when(sends)
        def _():
            by_sides(wait)

    @pl.when(first)
    def _():
        def wait(count):
            if count:
                arrived(inbox.at[:, : REACH * count], seed_sem)

        by_sides(wait)


def solution(mesh):
    wins, secs = mesh.shape["win"], mesh.shape["sec"]

    def run(initial, props, screen, links, kinds, counts):
        fronts, local, sources, width = initial.shape
        coeffs = width // 2
        entries = props.shape[1]
        group = 8 if sources % 8 == 0 else sources
        smem = pl.BlockSpec(memory_space=pltpu.SMEM)
        vmem = pl.BlockSpec(memory_space=pltpu.VMEM)
        whole = pl.BlockSpec(memory_space=pl.ANY)
        lines = -(-(3 * entries + 2) // 8) * 8
        return pl.pallas_call(
            functools.partial(kernel, wins, secs, group),
            out_shape=pltpu.VMEM((1, fronts, local, sources, width), jnp.bfloat16),
            in_specs=[smem, smem, smem, vmem, whole, whole],
            out_specs=vmem,
            scratch_shapes=[
                pltpu.VMEM((fronts, local + 2 * REACH, sources, width), jnp.bfloat16),
                pltpu.VMEM((fronts, local + 2, sources, width), jnp.bfloat16),
                pltpu.VMEM((2, entries, coeffs, coeffs), jnp.bfloat16),
                pltpu.VMEM((2 * (local + 2) * group, entries * coeffs), jnp.bfloat16),
                pltpu.VMEM((local + 2, lines, coeffs), jnp.float32),
                pltpu.SemaphoreType.DMA((2,)),
                pltpu.SemaphoreType.DMA,
                pltpu.SemaphoreType.DMA((2,)),
                pltpu.SemaphoreType.DMA,
                pltpu.SemaphoreType.DMA((fronts * (sources // group),)),
            ],
            compiler_params=pltpu.CompilerParams(collective_id=0, has_side_effects=True),
            name="beamlets",
        )(links, kinds, counts, screen, initial, props[0])

    placed = (
        P(None, "win", None, None),
        P("sec", None, None, None, None),
        P("sec", "win", None),
        P("sec", "win", None),
        P("sec", "win", None),
        P("sec", "win"),
    )
    return jax.shard_map(
        run,
        mesh=mesh,
        in_specs=placed,
        out_specs=P("sec", None, "win", None, None),
        check_vma=False,
    )
```

time: 36.5 us -> 34.4 us (0.942)
  Pallas kernels: 35.6 us -> 33.5 us
    pallas_call x1, Pallas kernels: 35.6 us -> 33.5 us  [run(): pl.pallas_call(functools.partial(kernel, wins, secs, group), out_shape=pl...]
where the time goes in v1:
time: 34.4 us; the launch traced here: 34.2 us
  Pallas kernels  33.5 us (97%)
  local copies, waits for them, and re-layouts  0.7 us (2%)
    pallas_call x1, Pallas kernels, run(): pl.pallas_call(functools.partial(kernel, wins, secs, group), out_shape=pl...  33.5 us
    unnamed x1, local copies, waits for them, and re-layouts  0.7 us

profile of v1, /device:TPU:7, one launch (start us, length us, event | category | flops | bytes accessed | tf_op | source)
XLA Modules:
  0.0 34.2 jit_solution(876188945988933470)
XLA Ops:
  0.0 33.5 %beamlets.1 = bf16[1,5,2,24,512]{4,3,2,1,0:T(8,128)(2,1)S(1)} custom-call(s32[1,2,6]{2,1,0:T(2,128)} %links.1, s32[1,2,6]{2,1,0:T(2,128)} %kinds.1, s32[1,2]{1,0:T(1,128)} %counts.1, f32[1,2,256]{2,1,0:T(2,128)} %screen.1, bf16[5,2,24,512]{3,2,1,0:T(8,128)(2,1)} %initial.1, bf16[8,2,256,256]{3,2,1,0:T(8,128)(2,1)} %bitcast.1), custom_call_target="tpu_custom_call" | custom-call | tf_op jit(solution)/shard_map/beamlets/pallas_call | solution.py:302
  33.5 0.7 %copy.8 = bf16[1,5,2,24,512]{4,3,2,1,0:T(8,128)(2,1)} copy(bf16[1,5,2,24,512]{4,3,2,1,0:T(8,128)(2,1)S(1)} %beamlets.1) | data formatting | bytes 491520
